TPU v7x, 128 devices: a whole 4x4x4 slice. The times are simulated.
128 devices in a mesh: judge: 4 (over y_hi, core), fsdp: 32 (over y_lo, x, z).
Axes of the slice: x: 4, y: 4 (y_hi: 2, y_lo: 2; y = y_hi * 2 + y_lo), z: 4, core: 2. Of those that a mesh axis runs over, the one named last changes fastest.
Arguments:
- hidden: bfloat16 [4, 32768, 4096], P('judge', 'fsdp'), may hold values from -32 to 32
- lengths: int32 [64], replicated, may hold values from 128 to 512
- duplicate_group_index: int32 [64], replicated, may hold values from 0 to 15, as said below
- attn_gain: bfloat16 [4, 4096], P('judge', 'fsdp'), may hold values from 0.5 to 1.5
- w_query: bfloat16 [4, 4096, 4096], P('judge', None, 'fsdp'), may hold values from -1 to 1
- w_key: bfloat16 [4, 4096, 1024], P('judge', 'fsdp'), may hold values from -1 to 1
- w_value: bfloat16 [4, 4096, 1024], P('judge', 'fsdp'), may hold values from -0.09375 to 0.09375
- w_out: bfloat16 [4, 4096, 4096], P('judge', 'fsdp'), may hold values from -0.09375 to 0.09375
- mlp_gain: bfloat16 [4, 4096], P('judge', 'fsdp'), may hold values from 0.5 to 1.5
- w_gate: bfloat16 [4, 4096, 14336], P('judge', None, 'fsdp'), may hold values from -0.09375 to 0.09375
- w_up: bfloat16 [4, 4096, 14336], P('judge', None, 'fsdp'), may hold values from -0.09375 to 0.09375
- w_down: bfloat16 [4, 14336, 4096], P('judge', 'fsdp'), may hold values from -0.046875 to 0.046875
- final_gain: bfloat16 [4, 4096], P('judge', 'fsdp'), may hold values from 0.5 to 1.5
- reward_head: float32 [4, 4096], P('judge'), may hold values from -8 to 8
Outputs:
- survivor_weights: float32 [64], replicated
- cluster_features: float32 [16, 4096], P(None, 'fsdp')
Inputs may be any that keep to these rules, and one draw needn't show every extreme that they name: `duplicate_group_index`: every cluster holds exactly four candidates.
All inputs are finite; a program needn't handle non-finite values.
Results may differ from a plain program's by a relative error of at most 0.003.
Values may be sent and summed in bfloat16 or wider, within the bound.
No kernel may reach another device: no remote copies, remote signals or barrier semaphores. Data moves between devices by JAX's collectives and lax.ppermute only.
A program may use at most 192 MiB of HBM per device.

v0:
```python
import math
import jax
import jax.numpy as jnp
from jax import lax
from jax.sharding import PartitionSpec as P

KV_HEADS = 8
HEAD_DIM = 128
LEN = 512
EPS = 1e-05
ROPE_BASE = 500000.0


def in_order(blocks, dim):
    dims = list(blocks.shape[1:])
    dims[dim] *= blocks.shape[0]
    return jnp.moveaxis(blocks, 0, dim).reshape(dims)


def gather_packed(arrays, axis, dims):
    ravelled = jnp.concatenate([a.reshape(-1) for a in arrays])
    lines, at, done = (lax.all_gather(ravelled, axis), 0, [])
    for a, dim in zip(arrays, dims):
        blocks = lines[:, at : at + a.size].reshape(-1, *a.shape)
        done.append(in_order(blocks, dim))
        at += a.size
    return tuple(done)


def sent_together(arrays, axis, dim, along):
    both = jnp.concatenate(arrays, axis=along)
    filled, at, done = (lax.all_gather(both, axis, axis=dim, tiled=True), 0, [])
    for a in arrays:
        done.append(lax.slice_in_dim(filled, at, at + a.shape[along], axis=along))
        at += a.shape[along]
    return tuple(done)


def cut_along(x, dim, peers):
    before, after = (x.shape[:dim], x.shape[dim + 1 :])
    return jnp.moveaxis(x.reshape(*before, peers, -1, *after), dim, 0)


def sum_at_owner(x, axis, dim):
    peers = lax.axis_size(axis)
    blocks = lax.all_to_all(cut_along(x, dim, peers), axis, 0, 0, tiled=True)
    return jnp.sum(blocks, axis=0)


def rows_for(lines, peers):
    spare = -lines.shape[0] % peers
    if not spare:
        return lines
    return jnp.concatenate([lines, jnp.zeros((spare, *lines.shape[1:]), lines.dtype)])


def from_everyone(x, axis):
    peers = lax.axis_size(axis)
    return lax.all_to_all(jnp.broadcast_to(x[None], (peers, *x.shape)), axis, 0, 0, tiled=True)


def gather_directly(x, axis, dim):
    blocks = from_everyone(x, axis)
    return in_order(blocks, dim)


def total_of(x, axes):
    lines = x.reshape(-1, x.shape[-1])
    own = sum_at_owner(rows_for(lines, lax.axis_size(axes)), axes, 0)
    whole = gather_directly(own, axes, 0)
    return whole[: len(lines)].reshape(x.shape)


def taken_together(x, axis):
    return from_everyone(x, axis).sum(axis=0)


def packed_total(arrays, axis):
    ends = [0]
    for a in arrays:
        ends.append(ends[-1] + a.size)
    running = taken_together(jnp.concatenate([a.ravel() for a in arrays]), axis)
    return tuple((running[b:e].reshape(a.shape) for a, b, e in zip(arrays, ends, ends[1:])))


def row_scale(v):
    return lax.rsqrt(jnp.mean(v * v, axis=-1, keepdims=True) + EPS)


def angles(position):
    half = HEAD_DIM // 2
    freq = jnp.exp(jnp.arange(half, dtype=jnp.float32) * (-2.0 * math.log(ROPE_BASE) / HEAD_DIM))
    turned = position[..., None] * freq
    return (jnp.cos(turned), jnp.sin(turned))


def rotate(v, cosine, sine):
    half = HEAD_DIM // 2
    first = v[..., :half]
    second = v[..., half:]
    return jnp.concatenate(
        [first * cosine - second * sine, second * cosine + first * sine], axis=-1
    )


def remaining_candidates(judge_panel, duplicate_group_index, duplicate_groups):
    same = duplicate_group_index[:, None] == duplicate_group_index[None, :]
    top = jnp.max(jnp.where(same, judge_panel[None, :], -1e30), axis=1)
    expo = jnp.exp(judge_panel - top)
    total = jnp.sum(jnp.where(same, expo[None, :], 0.0), axis=1)
    weight_values = expo / total
    panel_member = (
        duplicate_group_index[:, None] == jnp.arange(duplicate_groups, dtype=jnp.int32)[None, :]
    ).astype(jnp.float32)
    return (weight_values, panel_member)


def body(
    hidden,
    lengths,
    duplicate_group_index,
    attn_gain,
    w_query,
    w_key,
    w_value,
    w_out,
    mlp_gain,
    w_gate,
    w_up,
    w_down,
    final_gain,
    reward_head,
):
    reward_judges = lax.axis_size("judge")
    devices = lax.axis_size("fsdp")
    me = lax.axis_index("fsdp")
    tokens = hidden[0]
    tok_dev, width = tokens.shape
    seq_dev = tok_dev // LEN
    cands = lengths.shape[0]
    duplicate_groups = cands // 4
    groups = width // HEAD_DIM // KV_HEADS
    column_count = width // devices
    col_start = me * column_count
    own_len = lax.dynamic_slice_in_dim(lengths, me * seq_dev, seq_dev)
    last_index = jnp.arange(seq_dev, dtype=jnp.int32) * LEN + own_len - 1
    own_last = tokens[last_index]
    x_last, gain_attn, gain_mlp = gather_packed(
        (own_last, attn_gain[0], mlp_gain[0]), "fsdp", (0, 0, 0)
    )
    gain_final = final_gain[0]
    x_last = x_last.astype(jnp.float32)
    scale = row_scale(tokens.astype(jnp.float32))
    key_rows, value_rows = sent_together((w_key[0], w_value[0]), "fsdp", 0, 1)
    tok_norm = (tokens.astype(jnp.float32) * scale * gain_attn.astype(jnp.float32)).astype(
        jnp.bfloat16
    )
    keys = jnp.dot(tok_norm, key_rows, preferred_element_type=jnp.float32)
    values = jnp.dot(tok_norm, value_rows, preferred_element_type=jnp.float32)
    key_cos, key_sin = angles(jnp.arange(LEN, dtype=jnp.float32))
    keys = keys.reshape(seq_dev, LEN, KV_HEADS, HEAD_DIM)
    keys = rotate(keys, key_cos[None, :, None, :], key_sin[None, :, None, :]).astype(jnp.bfloat16)
    values = values.astype(jnp.bfloat16).reshape(seq_dev, LEN, KV_HEADS, HEAD_DIM)
    q_norm = (x_last * row_scale(x_last) * gain_attn.astype(jnp.float32)).astype(jnp.bfloat16)
    q_part = jnp.dot(q_norm, w_query[0], preferred_element_type=jnp.float32)
    q_part = q_part.reshape(cands, q_part.shape[1] // HEAD_DIM, HEAD_DIM)
    cosine, sine = angles((lengths - 1).astype(jnp.float32))
    q_part = (
        rotate(q_part, cosine[:, None, :], sine[:, None, :]).astype(jnp.bfloat16).reshape(cands, -1)
    )
    q_own = lax.all_to_all(q_part, "fsdp", split_axis=0, concat_axis=1, tiled=True)
    q_own = q_own.reshape(seq_dev, KV_HEADS, groups, HEAD_DIM)
    scores = jnp.einsum(
        "skgd,slkd->skgl", q_own, keys, preferred_element_type=jnp.float32
    ) * HEAD_DIM ** (-0.5)
    valid = jnp.arange(LEN, dtype=jnp.int32)[None, None, None, :] < own_len[:, None, None, None]
    scores = jnp.where(valid, scores, -1e30)
    top = jnp.max(scores, axis=-1, keepdims=True)
    expo = jnp.exp(scores - top)
    probs = (expo / jnp.sum(expo, axis=-1, keepdims=True)).astype(jnp.bfloat16)
    mixed = jnp.einsum("skgl,slkd->skgd", probs, values, preferred_element_type=jnp.float32)
    mixed = mixed.reshape(seq_dev, width).astype(jnp.bfloat16)
    head_rows = lax.all_to_all(mixed, "fsdp", split_axis=1, concat_axis=0, tiled=True)
    attn = total_of(jnp.dot(head_rows, w_out[0], preferred_element_type=jnp.float32), "fsdp")
    after_attn = x_last + attn
    m_norm = (after_attn * row_scale(after_attn) * gain_mlp.astype(jnp.float32)).astype(
        jnp.bfloat16
    )
    gate = jnp.dot(m_norm, w_gate[0], preferred_element_type=jnp.float32)
    up = jnp.dot(m_norm, w_up[0], preferred_element_type=jnp.float32)
    act = (jax.nn.silu(gate) * up).astype(jnp.bfloat16)
    down_terms = jnp.dot(act, w_down[0], preferred_element_type=jnp.float32)
    down_cols = sum_at_owner(down_terms, "fsdp", 1)
    after_cols = lax.dynamic_slice_in_dim(after_attn, col_start, column_count, 1) + down_cols
    head_cols = lax.dynamic_slice_in_dim(reward_head[0], col_start, column_count, 0)
    weighted = after_cols * gain_final.astype(jnp.float32)
    squares, product = packed_total(
        (
            jnp.sum(after_cols * after_cols, axis=1),
            jnp.dot(weighted, head_cols, precision=lax.Precision.HIGHEST),
        ),
        "fsdp",
    )
    col_scale = lax.rsqrt(squares / width + EPS)
    feature_cols = weighted * col_scale[:, None]
    score = product * col_scale
    total_cols, score_total = packed_total((feature_cols, score), "judge")
    weight_values, panel_member = remaining_candidates(
        score_total / reward_judges, duplicate_group_index, duplicate_groups
    )
    cluster_cols = jnp.dot(
        panel_member.T,
        weight_values[:, None] * (total_cols / reward_judges),
        precision=lax.Precision.HIGHEST,
    )
    return (weight_values, cluster_cols)


def solution(mesh):
    in_specs = (
        P("judge", "fsdp", None),
        P(),
        P(),
        P("judge", "fsdp"),
        P("judge", None, "fsdp"),
        P("judge", "fsdp", None),
        P("judge", "fsdp", None),
        P("judge", "fsdp", None),
        P("judge", "fsdp"),
        P("judge", None, "fsdp"),
        P("judge", None, "fsdp"),
        P("judge", "fsdp", None),
        P("judge", "fsdp"),
        P("judge", None),
    )
    out_specs = (P(), P(None, "fsdp"))
    return jax.shard_map(body, mesh=mesh, in_specs=in_specs, out_specs=out_specs, check_vma=False)
```

profile of v0, /device:TPU:1, one launch (start us, length us, event | category | flops | bytes accessed | tf_op | source)
XLA Modules:
  0.0 385.3 jit_solution(3134053307039716645)
XLA Ops:
  7.2 2.0 pad_maximum_fusion
  10.0 5.0 %gather_fusion = bf16[2,4096]{1,0:T(2,128)(2,1)S(1)} fusion(bf16[1024,4096]{1,0:T(8,128)(2,1)} %bitcast.116, s32[1024]{0:T(1024)S(1)} %pad_clamp_fusion), kind=kCustom, calls=%fused_computation | custom fusion | bytes 32776 | tf_op jit(solution)/shard_map/gather | solution.py:147
  15.8 93.5 %all-gather.1 = bf16[32,1,8448]{2,1,0:T(2,128)(2,1)S(1)} all-gather(bf16[1,1,8448]{2,1,0:T(2,128)(2,1)S(1)} %reshape.357), channel_id=2, replica_groups=mesh['judge'=4,'fsdp'=32] {'fsdp'}, dimensions={0}, use_global_device_ids=true | all-gather | bytes 557568 | tf_op jit(solution)/shard_map/all_gather | solution.py:22
  109.4 1.1 reshape.342
  110.6 1.4 multiply_reduce_fusion.1
  113.4 1.6 convolution_bitcast_fusion
  115.9 4.0 %all-to-all-start = ((bf16[32,2,128]{2,1,0:T(2,128)(2,1)}), bf16[32,2,128]{2,1,0:T(2,128)(2,1)S(1)}, u32[]{:S(2)}, u32[]{:S(2)}) async-start(bf16[32,2,128]{2,1,0:T(2,128)(2,1)} %pad_maximum_fusion.3), calls=%async_computation | async-start | bytes 32768 | tf_op jit(solution)/shard_map/all_to_all | solution.py:171
  119.9 5.2 %fusion.1 = f32[1024]{0:T(1024)S(1)} fusion(bf16[1,1024,4096]{2,1,0:T(8,128)(2,1)} %param.14), kind=kLoop, calls=%fused_computation.4 | loop fusion | flops 12581888 | bytes 8392704 | tf_op jit(solution)/shard_map/reduce_sum | solution.py:87
  125.6 10.4 %multiply_convert_fusion = bf16[1,1024,4096]{2,1,0:T(8,128)(2,1)} fusion(bf16[1,1024,4096]{2,1,0:T(8,128)(2,1)} %param.14, f32[4096]{0:T(1024)S(1)} %get-tuple-element.13, f32[1024]{0:T(1024)S(1)} %add_rsqrt_fusion.1), kind=kLoop, calls=%fused_computation.7 | loop fusion | flops 16777216 | bytes 16797696 | tf_op jit(solution)/shard_map/convert_element_type | solution.py:155
  136.1 77.0 %all-gather.4.cloned.1.call-done = bf16[4096,2048]{1,0:T(8,128)(2,1)} async-done(((bf16[128,2048]{1,0:T(8,128)(2,1)}), bf16[4096,2048]{1,0:T(8,128)(2,1)}) %all-gather.4.cloned.1.call-update) | async-done | bytes 16777232 | tf_op jit(solution)/shard_map/all_gather | solution.py:32
  213.1 7.6 %slice_bitcast_fusion = bf16[1024,4096]{0,1:T(8,128)(2,1)} fusion(bf16[4096,2048]{1,0:T(8,128)(2,1)} %all-gather.4.cloned.1.call-done), kind=kLoop, calls=%fused_computation.10 | loop fusion | bytes 16777216 | tf_op jit(solution)/shard_map/dot_general | solution.py:158
  220.7 12.0 %copy.43 = bf16[1024,4096]{1,0:T(8,128)(2,1)} copy(bf16[1024,4096]{0,1:T(8,128)(2,1)} %slice_bitcast_fusion) | data formatting | bytes 16777216 | tf_op jit(solution)/shard_map/dot_general | solution.py:158
  232.7 13.9 %convert_bitcast_fusion = bf16[128,8,8,128]{3,1,2,0:T(8,128)(2,1)S(1)} fusion(bf16[4096,2048]{1,0:T(8,128)(2,1)} %all-gather.4.cloned.1.call-done, f32[4096]{0:T(1024)S(1)} %get-tuple-element.13, f32[1024]{0:T(1024)S(1)} %add_rsqrt_fusion.1, bf16[1,1024,4096]{2,1,0:T(8,128)(2,1)} %param.14), kind=kOutput, calls=%fused_computation.26 | convolution fusion | flops 8607760384 | bytes 18894848 | tf_op jit(solution)/shard_map/dot_general | solution.py:159
  246.6 2.0 copy.62
  248.6 11.4 %fusion.103 = f32[2,512,8,128]{1,3,2,0:T(8,128)S(1)} fusion(bf16[2,512,4096,1]{2,1,3,0:T(8,128)(2,1)} %bitcast.117, bf16[8,128,4096,1]{2,1,0,3:T(8,128)(2,1)S(1)} %bitcast.118), kind=kOutput, calls=%fused_computation.122 | convolution fusion | flops 8589934592 | bytes 20971520 | tf_op jit(solution)/shard_map/dot_general | solution.py:158
  260.0 1.7 subtract_convert_fusion
  261.8 1.8 fusion.100
  263.5 2.1 fusion.46
  265.7 11.7 %all_to_all.53 = bf16[2,32,128]{2,0,1:T(2,128)(2,1)S(1)} all-to-all(bf16[2,32,128]{2,0,1:T(2,128)(2,1)S(1)} %copy.46), channel_id=1, replica_groups=mesh['judge'=4,'fsdp'=32] {'fsdp'}, dimensions={1} | all-to-all | bytes 32768 | tf_op jit(solution)/shard_map/all_to_all | solution.py:183
  278.5 15.5 %all_to_all.54 = f32[32,2,4096]{2,1,0:T(2,128)S(1)} all-to-all(f32[32,2,4096]{2,1,0:T(2,128)S(1)} %copy.48), channel_id=1, replica_groups=mesh['judge'=4,'fsdp'=32] {'fsdp'}, dimensions={0} | all-to-all | bytes 2097152 | tf_op jit(solution)/shard_map/all_to_all | solution.py:46
  294.4 1.5 broadcast_in_dim.39
  295.9 7.1 %all-to-all-start.3 = ((f32[32,2,4096]{2,1,0:T(2,128)}), f32[32,2,4096]{2,1,0:T(2,128)S(1)}, u32[]{:S(2)}, u32[]{:S(2)}) async-start(f32[32,2,4096]{2,1,0:T(2,128)} %broadcast_in_dim.39), calls=%async_computation.3 | async-start | bytes 2097152 | tf_op jit(solution)/shard_map/all_to_all | solution.py:59
  303.0 1.9 reshape.344
  304.9 11.8 %all-to-all-done.3 = f32[32,2,4096]{2,1,0:T(2,128)S(1)} async-done(((f32[32,2,4096]{2,1,0:T(2,128)}), f32[32,2,4096]{2,1,0:T(2,128)S(1)}, u32[]{:S(2)}, u32[]{:S(2)}) %all-to-all-start.3) | async-done | bytes 1048608 | tf_op jit(solution)/shard_map/all_to_all | solution.py:59
  316.7 2.0 multiply_reduce_fusion
  319.5 3.2 fusion.14
  322.7 6.3 %fusion.26 = f32[32,64,128]{2,1,0:T(8,128)} fusion(bf16[64,4096]{1,0:T(8,128)(2,1)S(1)} %convert_element_type.126, bf16[1,4096,448]{1,2,0:T(8,128)(2,1)} %param.24, f32[64,448]{1,0:T(8,128)S(1)} %fusion.14, bf16[1,448,4096]{2,1,0:T(8,128)(2,1)} %param.25), kind=kOutput, calls=%fused_computation.29 | convolution fusion | flops 469934080 | bytes 9027584 | tf_op jit(solution)/shard_map/dot_general | solution.py:192
  329.0 6.7 %all-to-all-start.4 = ((f32[32,64,128]{2,1,0:T(8,128)}), f32[32,64,128]{2,1,0:T(8,128)S(1)}, u32[]{:S(2)}, u32[]{:S(2)}) async-start(f32[32,64,128]{2,1,0:T(8,128)} %fusion.26), calls=%async_computation.4 | async-start | bytes 2097152 | tf_op jit(solution)/shard_map/all_to_all | solution.py:46
  335.8 1.7 reshape.339
  337.5 13.1 %all-to-all-done.4 = f32[32,64,128]{2,1,0:T(8,128)S(1)} async-done(((f32[32,64,128]{2,1,0:T(8,128)}), f32[32,64,128]{2,1,0:T(8,128)S(1)}, u32[]{:S(2)}, u32[]{:S(2)}) %all-to-all-start.4) | async-done | bytes 1048608 | tf_op jit(solution)/shard_map/all_to_all | solution.py:46
  352.5 12.5 %all_to_all.55 = f32[32,1,128]{2,1,0:T(1,128)S(1)} all-to-all(f32[32,1,128]{2,1,0:T(1,128)S(1)} %broadcast_in_dim.40), channel_id=1, replica_groups=mesh['judge'=4,'fsdp'=32] {'fsdp'}, dimensions={0} | all-to-all | bytes 32768 | tf_op jit(solution)/shard_map/all_to_all | solution.py:59
  365.3 11.2 %all_to_all.56 = f32[4,1,8256]{2,1,0:T(1,128)S(1)} all-to-all(f32[4,1,8256]{2,1,0:T(1,128)S(1)} %broadcast_in_dim.41), channel_id=1, replica_groups=mesh['judge'=4,'fsdp'=32] {'judge'}, dimensions={0} | all-to-all | bytes 264192 | tf_op jit(solution)/shard_map/all_to_all | solution.py:59
  (62 shorter events, 10.9 us)
Async XLA Ops:
  7.2 270.2 %copy-start = (bf16[1,128,4096]{2,1,0:T(8,128)(2,1)S(1)}, bf16[1,128,4096]{2,1,0:T(8,128)(2,1)}, u32[]{:S(2)}) copy-start(bf16[1,128,4096]{2,1,0:T(8,128)(2,1)} %param.21) | copy-start | bytes 3145732
  7.2 206.0 %all-gather.4.cloned.1.call-start = ((), (), s32[]{:S(2)}) async-start(), calls=%async_computation.7 | async-start | bytes 17301504 | tf_op jit(solution)/shard_map/all_gather | solution.py:32
  112.0 3.0 copy-start.3
  115.9 20.2 %all-to-all-start = ((bf16[32,2,128]{2,1,0:T(2,128)(2,1)}), bf16[32,2,128]{2,1,0:T(2,128)(2,1)S(1)}, u32[]{:S(2)}, u32[]{:S(2)}) async-start(bf16[32,2,128]{2,1,0:T(2,128)(2,1)} %pad_maximum_fusion.3), calls=%async_computation | async-start | bytes 32768 | tf_op jit(solution)/shard_map/all_to_all | solution.py:171
  232.7 15.9 %copy-start.1 = (bf16[1024,4096]{1,0:T(8,128)(2,1)S(1)}, bf16[1024,4096]{1,0:T(8,128)(2,1)}, u32[]{:S(2)}) copy-start(bf16[1024,4096]{1,0:T(8,128)(2,1)} %copy.43) | copy-start | bytes 25165828
  295.9 20.8 %all-to-all-start.3 = ((f32[32,2,4096]{2,1,0:T(2,128)}), f32[32,2,4096]{2,1,0:T(2,128)S(1)}, u32[]{:S(2)}, u32[]{:S(2)}) async-start(f32[32,2,4096]{2,1,0:T(2,128)} %broadcast_in_dim.39), calls=%async_computation.3 | async-start | bytes 2097152 | tf_op jit(solution)/shard_map/all_to_all | solution.py:59
  322.7 13.1 %copy-start.4 = (bf16[1,128]{1,0:T(2,128)(2,1)S(1)}, bf16[1,128]{1,0:T(2,128)(2,1)}, u32[]{:S(2)}) copy-start(bf16[1,128]{1,0:T(2,128)(2,1)} %param.26) | copy-start | bytes 772
  329.0 47.6 %copy-start.2 = (s32[64]{0:T(128)S(1)}, s32[64]{0:T(128)}, u32[]{:S(2)}) copy-start(s32[64]{0:T(128)} %param.16) | copy-start | bytes 772
  329.0 21.6 %all-to-all-start.4 = ((f32[32,64,128]{2,1,0:T(8,128)}), f32[32,64,128]{2,1,0:T(8,128)S(1)}, u32[]{:S(2)}, u32[]{:S(2)}) async-start(f32[32,64,128]{2,1,0:T(8,128)} %fusion.26), calls=%async_computation.4 | async-start | bytes 2097152 | tf_op jit(solution)/shard_map/all_to_all | solution.py:46
Sparse Core Ops, SparseCore 0:
  9.6 203.4 all-gather.3
where the time goes:
time: 387 us; the launch traced here: 385 us
  blocking collectives  145 us (37%)
  waiting for transfers between devices  102 us (26%)
  matrix products  42.3 us (11%)
  local copies, waits for them, and re-layouts  35.3 us (9%)
  other arithmetic  29.1 us (8%)
  starting transfers between devices  17.9 us (5%)
  between operations  14.4 us (4%)
    all_gather x1, blocking collectives, gather_packed(): lines, at, done = (lax.all_gather(ravelled, axis), 0, [])  93.5 us
    all_gather x1, waiting for transfers between devices, sent_together(): filled, at, done = (lax.all_gather(both, axis, axis=dim, tiled=True), 0, [])  77 us
    all_to_all x2, blocking collectives, from_everyone(): lax.all_to_all(jnp.broadcast_to(x[None], (peers, *x.shape)), axis, 0, 0,...  23.8 us
    dot_general x2, local copies, waits for them, and re-layouts, body(): keys = jnp.dot(tok_norm, key_rows, preferred_element_type=jnp.float32)  19.5 us
    all_to_all x1, blocking collectives, sum_at_owner(): blocks = lax.all_to_all(cut_along(x, dim, peers), axis, 0, 0, tiled=True)  15.5 us
    dot_general x1, matrix products, body(): values = jnp.dot(tok_norm, value_rows, preferred_element_type=jnp.float32)  13.9 us
    all_to_all x1, waiting for transfers between devices, sum_at_owner(): blocks = lax.all_to_all(cut_along(x, dim, peers), axis, 0, 0, tiled=True)  13.1 us
    all_to_all x1, waiting for transfers between devices, from_everyone(): lax.all_to_all(jnp.broadcast_to(x[None], (peers, *x.shape)), axis, 0, 0,...  11.8 us
  transfers between devices with their start and end apart: 4, of which 3 were waited for; matrix products, arithmetic and copies ran while one was open for 9% of the time, Pallas kernels for 0%

commit v1 on v0

--- a/solution.py
+++ b/solution.py
@@ -180,7 +180,10 @@
     probs = (expo / jnp.sum(expo, axis=-1, keepdims=True)).astype(jnp.bfloat16)
     mixed = jnp.einsum("skgl,slkd->skgd", probs, values, preferred_element_type=jnp.float32)
     mixed = mixed.reshape(seq_dev, width).astype(jnp.bfloat16)
-    head_rows = lax.all_to_all(mixed, "fsdp", split_axis=1, concat_axis=0, tiled=True)
+    size = lax.axis_size("fsdp")
+    pieces = jnp.stack(jnp.split(mixed, size, axis=1), axis=0)
+    pieces = lax.all_to_all(pieces, "fsdp", split_axis=0, concat_axis=0)
+    head_rows = jnp.concatenate(pieces, axis=0)
     attn = total_of(jnp.dot(head_rows, w_out[0], preferred_element_type=jnp.float32), "fsdp")
     after_attn = x_last + attn
     m_norm = (after_attn * row_scale(after_attn) * gain_mlp.astype(jnp.float32)).astype(

time: 387 us -> 389 us (level)
  transfers between devices with their start and end apart: 4 -> 4, of which waited for: 3 -> 3; matrix products, arithmetic and copies ran while one was open for 9% -> 8% of each run, Pallas kernels for 0% -> 0%
where the time goes in v1:
time: 389 us; the launch traced here: 388 us
  blocking collectives  145 us (37%)
  waiting for transfers between devices  102 us (26%)
  matrix products  42.3 us (11%)
  local copies, waits for them, and re-layouts  36.6 us (9%)
  other arithmetic  29.8 us (8%)
  starting transfers between devices  17.9 us (5%)
  between operations  14.5 us (4%)
    all_gather x1, blocking collectives, gather_packed(): lines, at, done = (lax.all_gather(ravelled, axis), 0, [])  93.5 us
    all_gather x1, waiting for transfers between devices, sent_together(): filled, at, done = (lax.all_gather(both, axis, axis=dim, tiled=True), 0, [])  77 us
    all_to_all x2, blocking collectives, from_everyone(): lax.all_to_all(jnp.broadcast_to(x[None], (peers, *x.shape)), axis, 0, 0,...  23.8 us
    dot_general x2, local copies, waits for them, and re-layouts, body(): keys = jnp.dot(tok_norm, key_rows, preferred_element_type=jnp.float32)  19.5 us
    all_to_all x1, blocking collectives, sum_at_owner(): blocks = lax.all_to_all(cut_along(x, dim, peers), axis, 0, 0, tiled=True)  15.5 us
    dot_general x1, matrix products, body(): values = jnp.dot(tok_norm, value_rows, preferred_element_type=jnp.float32)  13.9 us
    all_to_all x1, waiting for transfers between devices, sum_at_owner(): blocks = lax.all_to_all(cut_along(x, dim, peers), axis, 0, 0, tiled=True)  13.1 us
    all_to_all x1, waiting for transfers between devices, from_everyone(): lax.all_to_all(jnp.broadcast_to(x[None], (peers, *x.shape)), axis, 0, 0,...  11.8 us
  transfers between devices with their start and end apart: 4, of which 3 were waited for; matrix products, arithmetic and copies ran while one was open for 8% of the time, Pallas kernels for 0%

profile of v1, /device:TPU:1, one launch (start us, length us, event | category | flops | bytes accessed | tf_op | source)
XLA Modules:
  0.0 387.5 jit_solution(8945673412101251983)
XLA Ops:
  7.2 2.0 pad_maximum_fusion
  10.0 5.0 %gather_fusion = bf16[2,4096]{1,0:T(2,128)(2,1)S(1)} fusion(bf16[1024,4096]{1,0:T(8,128)(2,1)} %bitcast.242, s32[1024]{0:T(1024)S(1)} %pad_clamp_fusion), kind=kCustom, calls=%fused_computation | custom fusion | bytes 32776 | tf_op jit(solution)/shard_map/gather | solution.py:147
  15.8 93.5 %all-gather.1 = bf16[32,1,8448]{2,1,0:T(2,128)(2,1)S(1)} all-gather(bf16[1,1,8448]{2,1,0:T(2,128)(2,1)S(1)} %reshape_bitcast_fusion), channel_id=2, replica_groups=mesh['judge'=4,'fsdp'=32] {'fsdp'}, dimensions={0}, use_global_device_ids=true | all-gather | bytes 557568 | tf_op jit(solution)/shard_map/all_gather | solution.py:22
  110.6 1.4 multiply_reduce_fusion.1
  113.4 1.6 convolution_bitcast_fusion
  115.9 4.0 %all-to-all-start = ((bf16[32,2,128]{2,1,0:T(2,128)(2,1)}), bf16[32,2,128]{2,1,0:T(2,128)(2,1)S(1)}, u32[]{:S(2)}, u32[]{:S(2)}) async-start(bf16[32,2,128]{2,1,0:T(2,128)(2,1)} %pad_maximum_fusion.3), calls=%async_computation | async-start | bytes 32768 | tf_op jit(solution)/shard_map/all_to_all | solution.py:171
  119.9 5.2 %fusion.1 = f32[1024]{0:T(1024)S(1)} fusion(bf16[1,1024,4096]{2,1,0:T(8,128)(2,1)} %param.14), kind=kLoop, calls=%fused_computation.4 | loop fusion | flops 12581888 | bytes 8392704 | tf_op jit(solution)/shard_map/reduce_sum | solution.py:87
  125.6 10.4 %multiply_convert_fusion = bf16[1,1024,4096]{2,1,0:T(8,128)(2,1)} fusion(bf16[1,1024,4096]{2,1,0:T(8,128)(2,1)} %param.14, f32[4096]{0:T(1024)S(1)} %get-tuple-element.13, f32[1024]{0:T(1024)S(1)} %add_rsqrt_fusion.1), kind=kLoop, calls=%fused_computation.7 | loop fusion | flops 16777216 | bytes 16797696 | tf_op jit(solution)/shard_map/convert_element_type | solution.py:155
  136.1 77.0 %all-gather.4.cloned.1.call-done = bf16[4096,2048]{1,0:T(8,128)(2,1)} async-done(((bf16[128,2048]{1,0:T(8,128)(2,1)}), bf16[4096,2048]{1,0:T(8,128)(2,1)}) %all-gather.4.cloned.1.call-update) | async-done | bytes 16777232 | tf_op jit(solution)/shard_map/all_gather | solution.py:32
  213.1 7.6 %slice_bitcast_fusion = bf16[1024,4096]{0,1:T(8,128)(2,1)} fusion(bf16[4096,2048]{1,0:T(8,128)(2,1)} %all-gather.4.cloned.1.call-done), kind=kLoop, calls=%fused_computation.10 | loop fusion | bytes 16777216 | tf_op jit(solution)/shard_map/dot_general | solution.py:158
  220.7 12.0 %copy.1187 = bf16[1024,4096]{1,0:T(8,128)(2,1)} copy(bf16[1024,4096]{0,1:T(8,128)(2,1)} %slice_bitcast_fusion) | data formatting | bytes 16777216 | tf_op jit(solution)/shard_map/dot_general | solution.py:158
  232.7 13.9 %convert_bitcast_fusion = bf16[128,8,8,128]{3,1,2,0:T(8,128)(2,1)S(1)} fusion(bf16[4096,2048]{1,0:T(8,128)(2,1)} %all-gather.4.cloned.1.call-done, f32[4096]{0:T(1024)S(1)} %get-tuple-element.13, f32[1024]{0:T(1024)S(1)} %add_rsqrt_fusion.1, bf16[1,1024,4096]{2,1,0:T(8,128)(2,1)} %param.14), kind=kOutput, calls=%fused_computation.26 | convolution fusion | flops 8607760384 | bytes 18894848 | tf_op jit(solution)/shard_map/dot_general | solution.py:159
  246.6 2.0 copy.1205
  248.6 11.4 %fusion.102 = f32[2,512,8,128]{1,3,2,0:T(8,128)S(1)} fusion(bf16[2,512,4096,1]{2,1,3,0:T(8,128)(2,1)} %bitcast.243, bf16[8,128,4096,1]{2,1,0,3:T(8,128)(2,1)S(1)} %bitcast.244), kind=kOutput, calls=%fused_computation.186 | convolution fusion | flops 8589934592 | bytes 20971520 | tf_op jit(solution)/shard_map/dot_general | solution.py:158
  260.0 1.7 subtract_convert_fusion
  261.8 1.8 fusion.99
  263.5 2.1 fusion.46
  266.0 11.7 %all_to_all.45 = bf16[32,2,128]{2,1,0:T(2,128)(2,1)S(1)} all-to-all(bf16[32,2,128]{2,1,0:T(2,128)(2,1)S(1)} %constant_dynamic-update-slice_fusion), channel_id=1, replica_groups=mesh['judge'=4,'fsdp'=32] {'fsdp'}, dimensions={0} | all-to-all | bytes 32768 | tf_op jit(solution)/shard_map/all_to_all | solution.py:185
  278.9 15.5 %all_to_all.46 = f32[32,2,4096]{2,1,0:T(2,128)S(1)} all-to-all(f32[32,2,4096]{2,1,0:T(2,128)S(1)} %copy.1191), channel_id=1, replica_groups=mesh['judge'=4,'fsdp'=32] {'fsdp'}, dimensions={0} | all-to-all | bytes 2097152 | tf_op jit(solution)/shard_map/all_to_all | solution.py:46
  294.8 1.5 broadcast_in_dim.39
  296.3 7.1 %all-to-all-start.3 = ((f32[32,2,4096]{2,1,0:T(2,128)}), f32[32,2,4096]{2,1,0:T(2,128)S(1)}, u32[]{:S(2)}, u32[]{:S(2)}) async-start(f32[32,2,4096]{2,1,0:T(2,128)} %broadcast_in_dim.39), calls=%async_computation.3 | async-start | bytes 2097152 | tf_op jit(solution)/shard_map/all_to_all | solution.py:59
  303.4 1.9 reshape.341
  305.3 11.8 %all-to-all-done.3 = f32[32,2,4096]{2,1,0:T(2,128)S(1)} async-done(((f32[32,2,4096]{2,1,0:T(2,128)}), f32[32,2,4096]{2,1,0:T(2,128)S(1)}, u32[]{:S(2)}, u32[]{:S(2)}) %all-to-all-start.3) | async-done | bytes 1048608 | tf_op jit(solution)/shard_map/all_to_all | solution.py:59
  317.0 2.0 multiply_reduce_fusion
  319.0 1.4 multiply_convert_fusion.1
  321.7 3.2 fusion.14
  324.9 6.3 %fusion.26 = f32[32,64,128]{2,1,0:T(8,128)} fusion(bf16[64,4096]{1,0:T(8,128)(2,1)S(1)} %convert_element_type.125, bf16[1,4096,448]{1,2,0:T(8,128)(2,1)} %param.24, f32[64,448]{1,0:T(8,128)S(1)} %fusion.14, bf16[1,448,4096]{2,1,0:T(8,128)(2,1)} %param.25), kind=kOutput, calls=%fused_computation.29 | convolution fusion | flops 469934080 | bytes 9027584 | tf_op jit(solution)/shard_map/dot_general | solution.py:195
  331.2 6.7 %all-to-all-start.4 = ((f32[32,64,128]{2,1,0:T(8,128)}), f32[32,64,128]{2,1,0:T(8,128)S(1)}, u32[]{:S(2)}, u32[]{:S(2)}) async-start(f32[32,64,128]{2,1,0:T(8,128)} %fusion.26), calls=%async_computation.4 | async-start | bytes 2097152 | tf_op jit(solution)/shard_map/all_to_all | solution.py:46
  338.0 1.7 reshape.336
  339.7 13.1 %all-to-all-done.4 = f32[32,64,128]{2,1,0:T(8,128)S(1)} async-done(((f32[32,64,128]{2,1,0:T(8,128)}), f32[32,64,128]{2,1,0:T(8,128)S(1)}, u32[]{:S(2)}, u32[]{:S(2)}) %all-to-all-start.4) | async-done | bytes 1048608 | tf_op jit(solution)/shard_map/all_to_all | solution.py:46
  354.7 12.5 %all_to_all.47 = f32[32,1,128]{2,1,0:T(1,128)S(1)} all-to-all(f32[32,1,128]{2,1,0:T(1,128)S(1)} %broadcast_in_dim.40), channel_id=1, replica_groups=mesh['judge'=4,'fsdp'=32] {'fsdp'}, dimensions={0} | all-to-all | bytes 32768 | tf_op jit(solution)/shard_map/all_to_all | solution.py:59
  367.5 11.2 %all_to_all.48 = f32[4,1,8256]{2,1,0:T(1,128)S(1)} all-to-all(f32[4,1,8256]{2,1,0:T(1,128)S(1)} %broadcast_in_dim.41), channel_id=1, replica_groups=mesh['judge'=4,'fsdp'=32] {'judge'}, dimensions={0} | all-to-all | bytes 264192 | tf_op jit(solution)/shard_map/all_to_all | solution.py:59
  (94 shorter events, 12.7 us)
Async XLA Ops:
  7.2 270.6 %copy-start = (bf16[1,128,4096]{2,1,0:T(8,128)(2,1)S(1)}, bf16[1,128,4096]{2,1,0:T(8,128)(2,1)}, u32[]{:S(2)}) copy-start(bf16[1,128,4096]{2,1,0:T(8,128)(2,1)} %param.21) | copy-start | bytes 3145732
  7.2 206.0 %all-gather.4.cloned.1.call-start = ((), (), s32[]{:S(2)}) async-start(), calls=%async_computation.7 | async-start | bytes 17301504 | tf_op jit(solution)/shard_map/all_gather | solution.py:32
  112.0 3.0 copy-start.3
  115.9 20.2 %all-to-all-start = ((bf16[32,2,128]{2,1,0:T(2,128)(2,1)}), bf16[32,2,128]{2,1,0:T(2,128)(2,1)S(1)}, u32[]{:S(2)}, u32[]{:S(2)}) async-start(bf16[32,2,128]{2,1,0:T(2,128)(2,1)} %pad_maximum_fusion.3), calls=%async_computation | async-start | bytes 32768 | tf_op jit(solution)/shard_map/all_to_all | solution.py:171
  232.7 15.9 %copy-start.1 = (bf16[1024,4096]{1,0:T(8,128)(2,1)S(1)}, bf16[1024,4096]{1,0:T(8,128)(2,1)}, u32[]{:S(2)}) copy-start(bf16[1024,4096]{1,0:T(8,128)(2,1)} %copy.1187) | copy-start | bytes 25165828
  296.3 20.8 %all-to-all-start.3 = ((f32[32,2,4096]{2,1,0:T(2,128)}), f32[32,2,4096]{2,1,0:T(2,128)S(1)}, u32[]{:S(2)}, u32[]{:S(2)}) async-start(f32[32,2,4096]{2,1,0:T(2,128)} %broadcast_in_dim.39), calls=%async_computation.3 | async-start | bytes 2097152 | tf_op jit(solution)/shard_map/all_to_all | solution.py:59
  324.9 13.1 %copy-start.4 = (bf16[1,128]{1,0:T(2,128)(2,1)S(1)}, bf16[1,128]{1,0:T(2,128)(2,1)}, u32[]{:S(2)}) copy-start(bf16[1,128]{1,0:T(2,128)(2,1)} %param.26) | copy-start | bytes 772
  331.2 47.6 %copy-start.2 = (s32[64]{0:T(128)S(1)}, s32[64]{0:T(128)}, u32[]{:S(2)}) copy-start(s32[64]{0:T(128)} %param.16) | copy-start | bytes 772
  331.2 21.6 %all-to-all-start.4 = ((f32[32,64,128]{2,1,0:T(8,128)}), f32[32,64,128]{2,1,0:T(8,128)S(1)}, u32[]{:S(2)}, u32[]{:S(2)}) async-start(f32[32,64,128]{2,1,0:T(8,128)} %fusion.26), calls=%async_computation.4 | async-start | bytes 2097152 | tf_op jit(solution)/shard_map/all_to_all | solution.py:46
Sparse Core Ops, SparseCore 0:
  9.6 203.4 all-gather.3
